TPU v7x, 32 devices: a whole 2x2x4 slice. The times are simulated.
32 devices in a mesh: fs: 8 (over z, x), pol: 4 (over y, core).
Axes of the slice: x: 2, y: 2, z: 4, core: 2. Of those that a mesh axis runs over, the one named last changes fastest.
Arguments:
- facets: bfloat16 [4, 64, 4096, 128], P('pol', 'fs'), may hold values from -6 to 6
- owners: int32 [64], replicated, may hold values from 0 to 7, as said below
- counts: int32 [64], replicated, may hold values from 1 to 8, as said below
- coords: float32 [2, 128, 8, 128], P(None, 'fs'), may hold values from 0 to 512
- station_ids: int32 [128, 8, 2, 128], P('fs'), may hold values from 0 to 511
- jones_table: float32 [8, 512], replicated, may hold values from -3 to 3
Outputs:
- predicted: float32 [4, 2, 128, 8, 128], P('pol', None, 'fs')
Inputs may be any that keep to these rules, and one draw needn't show every extreme that they name: `owners`: each fs index owns at most 16 subgrids, and some index owns exactly 16. `counts`: some subgrid has exactly 8 blocks.
All inputs are finite; a program needn't handle non-finite values.
Results may differ from a plain program's by a relative error of at most 0.0055.
Values may be sent and summed in bfloat16 or wider, within the bound.
A program may use at most 128 MiB of HBM per device.

v0:
```python
import functools
import math

import jax
import jax.numpy as jnp
from jax import lax
from jax.experimental import pallas as pl
from jax.experimental.pallas import tpu as pltpu
from jax.sharding import PartitionSpec as P

R = 8
W = 64
S = 64
FH = 4096
SG = 512
UNROLL = 2
GROUP = 2

SIN_COEFS = [
    (-1) ** i * (2.0 * math.pi) ** (2 * i + 1) / math.factorial(2 * i + 1) for i in range(9)
]
COS_COEFS = [(-1) ** i * (2.0 * math.pi) ** (2 * i) / math.factorial(2 * i) for i in range(10)]


def dft_tables(length):
    indices = jnp.arange(length, dtype=jnp.int32)
    phases = indices[:, None] * indices[None, :] % length
    angles = phases.astype(jnp.float32) * (2.0 * math.pi / length)
    return (jnp.cos(angles).astype(jnp.bfloat16), jnp.sin(angles).astype(jnp.bfloat16))


def turn_table(rows, cols, length):
    row_index = jnp.arange(rows, dtype=jnp.int32)
    col_index = jnp.arange(cols, dtype=jnp.int32)
    phases = row_index[:, None] * col_index[None, :] % length
    angles = phases.astype(jnp.float32) * (2.0 * math.pi / length)
    return (jnp.cos(angles), jnp.sin(angles))


def horner(coefs, square):
    total = jnp.full_like(square, coefs[-1])
    for coef in coefs[-2::-1]:
        total = total * square + coef
    return total


def phase(position, multiple):
    turns = position * (multiple * (1.0 / SG))
    turns = turns - jnp.floor(turns + 0.5)
    square = turns * turns
    return horner(COS_COEFS, square), horner(SIN_COEFS, square) * turns


def twice(left, right):
    return (left[0] * right[0] - left[1] * right[1], left[1] * right[0] + left[0] * right[1])


def turn_lanes(values, sign):
    return pltpu.roll(values, W, 1) * sign


def predict_kernel(
    facet_local, capacity, index_ref, owners_ref, counts_ref, coords_ref, first_ref, second_ref,
    turn_cos_ref, turn_sin_ref, strip_ref, out_ref,
    wide_ref, turned_ref, windows_ref, grid_ref, vis_ref, items_ref, loads_ref
):
    facet = pl.program_id(0)
    width = 2 * W
    lanes = lax.broadcasted_iota(jnp.int32, (1, width), 1)
    sign = jnp.where(lanes < W, 1.0, -1.0)

    def widen(i, carry):
        rows = pl.ds(pl.multiple_of(i * 256, 256), 256)
        wide_ref[rows, :] = strip_ref[0, rows, :].astype(jnp.float32)
        return carry

    lax.fori_loop(0, FH // 256, widen, 0)

    def first(i, carry):
        starts = [i * GROUP + u for u in range(GROUP)]
        data = jnp.concatenate(
            [wide_ref[pl.ds(n, W, stride=S), :].astype(jnp.bfloat16) for n in starts], axis=1
        )
        both = jnp.dot(first_ref[...], data, preferred_element_type=jnp.float32)
        for u, n in enumerate(starts):
            part = both[:, u * width : (u + 1) * width]
            rows = pl.ds(pl.multiple_of(n * W, W), W)
            tc, ts = turn_cos_ref[rows, :], turn_sin_ref[rows, :]
            straight = part[:W] * tc - part[W:] * ts
            crossed = part[W:] * tc + part[:W] * ts
            turned_ref[rows, :] = straight + turn_lanes(crossed, sign)
        return carry

    lax.fori_loop(0, S // GROUP, first, 0)

    def second(i, carry):
        starts = [i * GROUP + u for u in range(GROUP)]
        data = jnp.concatenate(
            [turned_ref[pl.ds(k, S, stride=W), :].astype(jnp.bfloat16) for k in starts], axis=1
        )
        both = jnp.dot(second_ref[...], data, preferred_element_type=jnp.float32)
        for u, k in enumerate(starts):
            part = both[:, u * width : (u + 1) * width]
            rows = pl.ds(pl.multiple_of(k * S, S), S)
            windows_ref[facet, rows, :] = part[:S] + turn_lanes(part[S:], sign)
        return carry

    lax.fori_loop(0, W // GROUP, second, 0)

    @pl.when(facet == facet_local - 1)
    def _():
        predict_all(
            facet_local, capacity, index_ref, owners_ref, counts_ref, coords_ref, windows_ref,
            grid_ref, vis_ref, items_ref, loads_ref
        )
        out_ref[...] = vis_ref[...].astype(jnp.bfloat16)


def predict_all(
    facet_local, capacity, index_ref, owners_ref, counts_ref, coords_ref, windows_ref,
    grid_ref, out_ref, items_ref, loads_ref
):
    device_count = out_ref.shape[0]
    max_blocks = out_ref.shape[3]
    uppers = facet_local // 2
    scale = 1.0 / (math.sqrt(FH) * SG)
    row_start = ((index_ref[0] * facet_local) // R * W - SG // 2).astype(jnp.float32)
    col_start = ((index_ref[0] * facet_local) % R * W - SG // 2).astype(jnp.float32)
    out_ref[...] = jnp.zeros_like(out_ref)

    def clear(i, carry):
        loads_ref[i] = 0
        return carry

    lax.fori_loop(0, device_count, clear, 0)

    def list_items(s, total):
        owner = owners_ref[s]
        load = loads_ref[owner]
        loads_ref[owner] = load + 1
        place = (s * device_count + owner) * capacity + load

        def add(b, t):
            items_ref[t] = place * max_blocks + b
            return t + 1

        return lax.fori_loop(0, counts_ref[s], add, total)

    total = lax.fori_loop(0, owners_ref.shape[0], list_items, 0)

    def pad(i, carry):
        items_ref[total + i] = items_ref[total - 1]
        return carry

    lax.fori_loop(0, UNROLL - 1, pad, 0)
    lane = out_ref.shape[4]
    ramp = lax.broadcasted_iota(jnp.int32, (8, lane), 0).astype(jnp.float32)

    def pack(s, carry):
        for f in range(facet_local):
            rows = slice(f // 2 * W, (f // 2 + 1) * W)
            cols = slice(f % 2 * 2 * W, (f % 2 + 1) * 2 * W)
            grid_ref[s, rows, cols] = windows_ref[f, pl.ds(s, W, stride=S), :].astype(
                jnp.bfloat16
            )
        return carry

    lax.fori_loop(0, S, pack, 0)

    def one(item):
        b = item % max_blocks
        place = item // max_blocks
        load = place % capacity
        owner = (place // capacity) % device_count
        s = place // (capacity * device_count)
        x = coords_ref[owner, 0, load, pl.ds(b, 1), :]
        y = coords_ref[owner, 1, load, pl.ds(b, 1), :]
        fine = phase(y, ramp)
        coarse = [phase(y, ramp * 8.0), phase(y, ramp * 8.0 + 64.0)]
        cos_rows, sin_rows, neg_rows = [], [], []
        for half in coarse:
            c, s_ = half
            cc, ss = twice(
                (c[:, None, :], s_[:, None, :]), (fine[0][None], fine[1][None])
            )
            cos_rows.append(cc.reshape(W, lane).astype(jnp.bfloat16))
            sin_rows.append(ss.reshape(W, lane).astype(jnp.bfloat16))
            neg_rows.append(-sin_rows[-1])
        table = jnp.concatenate(
            [
                jnp.concatenate([cos_rows[0], sin_rows[0], cos_rows[1], sin_rows[1]], axis=0),
                jnp.concatenate([neg_rows[0], cos_rows[0], neg_rows[1], cos_rows[1]], axis=0),
            ],
            axis=1,
        )
        grid = jnp.dot(grid_ref[s], table, preferred_element_type=jnp.float32)
        upper = phase(y, ramp * (2.0 * W) + col_start)
        row_coarse = phase(x, ramp * 8.0 + row_start)
        row_fine = phase(x, ramp)
        sum_real = jnp.zeros((8, lane), jnp.float32)
        sum_imag = jnp.zeros((8, lane), jnp.float32)
        for h in range(uppers):
            mixed = twice((upper[0][h : h + 1], upper[1][h : h + 1]), row_coarse)
            part = grid[h * W : (h + 1) * W].reshape(8, 8, 2 * lane)
            real, imag = part[:, :, :lane], part[:, :, lane:]
            mc, ms = mixed[0][:, None, :], mixed[1][:, None, :]
            sum_real = sum_real + jnp.sum(real * mc + imag * ms, axis=0)
            sum_imag = sum_imag + jnp.sum(imag * mc - real * ms, axis=0)
        fc, fs = row_fine
        vis_real = jnp.sum(sum_real * fc + sum_imag * fs, axis=0, keepdims=True) * scale
        vis_imag = jnp.sum(sum_imag * fc - sum_real * fs, axis=0, keepdims=True) * scale
        return owner, load, b, vis_real, vis_imag

    def step(i, carry):
        for owner, load, b, vis_real, vis_imag in [
            one(items_ref[i * UNROLL + u]) for u in range(UNROLL)
        ]:
            out_ref[owner, load, 0, pl.ds(b, 1), :] = vis_real
            out_ref[owner, load, 1, pl.ds(b, 1), :] = vis_imag
        return carry

    lax.fori_loop(0, (total + UNROLL - 1) // UNROLL, step, 0)


def predict(strips, owners, counts, coords, device_index):
    device_count, _, capacity, max_blocks, lane = coords.shape
    facet_local = strips.shape[0]
    smem = pl.BlockSpec(memory_space=pltpu.SMEM)
    whole = lambda *shape: pl.BlockSpec(shape, lambda f: (0,) * len(shape))
    first = jnp.concatenate(dft_tables(W), axis=0)
    second = jnp.concatenate(dft_tables(S), axis=0)
    turns = [
        jnp.broadcast_to(table.T[:, :, None], (S, W, 2 * W)).reshape(FH, 2 * W)
        for table in turn_table(W, S, FH)
    ]
    slots = (device_count, capacity, 2, max_blocks, lane)
    return pl.pallas_call(
        functools.partial(predict_kernel, facet_local, capacity),
        out_shape=jax.ShapeDtypeStruct(slots, jnp.bfloat16),
        grid=(facet_local,),
        in_specs=[
            smem, smem, smem,
            whole(*coords.shape),
            whole(2 * W, W),
            whole(2 * S, S),
            whole(FH, 2 * W),
            whole(FH, 2 * W),
            pl.BlockSpec((1, FH, 2 * W), lambda f: (f, 0, 0)),
        ],
        out_specs=whole(*slots),
        scratch_shapes=[
            pltpu.VMEM((FH, 2 * W), jnp.float32),
            pltpu.VMEM((FH, 2 * W), jnp.float32),
            pltpu.VMEM((facet_local, FH, 2 * W), jnp.float32),
            pltpu.VMEM((S, facet_local // 2 * W, 4 * W), jnp.bfloat16),
            pltpu.VMEM(slots, jnp.float32),
            pltpu.SMEM((owners.shape[0] * max_blocks + UNROLL,), jnp.int32),
            pltpu.SMEM((device_count,), jnp.int32),
        ],
        compiler_params=pltpu.CompilerParams(vmem_limit_bytes=58 * 2**20),
    )(device_index.reshape(1), owners, counts, coords, first, second, *turns, strips)


def add_up_kernel(device_count, in_ref, out_ref, arrived_ref, send_sem, recv_sem):
    me = lax.axis_index("fs")
    barrier = pltpu.get_barrier_semaphore()
    peers = [lax.rem(me + step, device_count) for step in range(1, device_count)]
    for peer in peers:
        pl.semaphore_signal(
            barrier, inc=1, device_id={"fs": peer}, device_id_type=pl.DeviceIdType.MESH
        )
    pl.semaphore_wait(barrier, device_count - 1)
    copies = []
    for i, peer in enumerate(peers):
        copy = pltpu.make_async_remote_copy(
            src_ref=in_ref.at[peer],
            dst_ref=arrived_ref.at[i],
            send_sem=send_sem.at[i],
            recv_sem=recv_sem.at[i],
            device_id={"fs": peer},
            device_id_type=pl.DeviceIdType.MESH,
        )
        copy.start()
        copies.append(copy)
    out_ref[...] = in_ref[me].astype(jnp.float32)
    for i, copy in enumerate(copies):
        copy.wait_recv()
        out_ref[...] += arrived_ref[i].astype(jnp.float32)
    for copy in copies:
        copy.wait_send()


def add_up(parts):
    device_count = parts.shape[0]
    vmem = pl.BlockSpec(memory_space=pltpu.VMEM)
    return pl.pallas_call(
        functools.partial(add_up_kernel, device_count),
        out_shape=jax.ShapeDtypeStruct(parts.shape[1:], jnp.float32),
        in_specs=[vmem],
        out_specs=vmem,
        scratch_shapes=[
            pltpu.VMEM((device_count - 1,) + parts.shape[1:], jnp.bfloat16),
            pltpu.SemaphoreType.DMA((device_count - 1,)),
            pltpu.SemaphoreType.DMA((device_count - 1,)),
        ],
        compiler_params=pltpu.CompilerParams(collective_id=0, has_side_effects=True),
    )(parts)


def correct_kernel(index_ref, owners_ref, counts_ref, left_ref, right_ref, table_ref, vis_ref, out_ref):
    capacity = out_ref.shape[1]
    max_blocks, lane = out_ref.shape[2:]
    chunks = table_ref.shape[1] // lane
    me = index_ref[0]
    out_ref[...] = jnp.zeros_like(out_ref)
    block = lax.broadcasted_iota(jnp.int32, (max_blocks, lane), 0)

    def look_up(first, ids):
        low = ids % lane
        high = ids // lane
        found = []
        for row in range(4):
            entry = None
            for chunk in range(chunks):
                source = jnp.broadcast_to(
                    table_ref[first + row : first + row + 1, chunk * lane : (chunk + 1) * lane],
                    (max_blocks, lane),
                )
                got = jnp.take_along_axis(source, low, axis=1, mode="promise_in_bounds")
                entry = got if entry is None else jnp.where(high == chunk, got, entry)
            found.append(entry)
        return [(found[0], found[1]), (found[2], found[3])]

    def product(a, b):
        return (a[0] * b[0] - a[1] * b[1], a[0] * b[1] + a[1] * b[0])

    def slot(s, load):
        is_mine = owners_ref[s] == me

        @pl.when(is_mine)
        def _():
            left = look_up(0, left_ref[load])
            right = look_up(4, right_ref[load])
            total_real = jnp.zeros((max_blocks, lane), jnp.float32)
            total_imag = jnp.zeros((max_blocks, lane), jnp.float32)
            for inner_row in range(2):
                for inner_col in range(2):
                    comp = 2 * inner_row + inner_col
                    step = product(
                        left[inner_row], (vis_ref[comp, load, 0], vis_ref[comp, load, 1])
                    )
                    step = product(step, (right[inner_col][0], -right[inner_col][1]))
                    total_real = total_real + step[0]
                    total_imag = total_imag + step[1]
            keep = block < counts_ref[s]
            out_ref[0, load] = jnp.where(keep, total_real, 0.0)
            out_ref[1, load] = jnp.where(keep, total_imag, 0.0)

        return load + is_mine.astype(jnp.int32)

    lax.fori_loop(0, owners_ref.shape[0], slot, 0)


def correct(visible, owners, counts, station_ids, tables, device_index):
    _, capacity, _, max_blocks, lane = visible.shape
    smem = pl.BlockSpec(memory_space=pltpu.SMEM)
    vmem = pl.BlockSpec(memory_space=pltpu.VMEM)
    return pl.pallas_call(
        correct_kernel,
        out_shape=jax.ShapeDtypeStruct((2, capacity, max_blocks, lane), jnp.float32),
        in_specs=[smem, smem, smem, vmem, vmem, vmem, vmem],
        out_specs=vmem,
    )(
        device_index.reshape(1),
        owners,
        counts,
        station_ids[:, :, 0, :],
        station_ids[:, :, 1, :],
        tables,
        visible,
    )


def on_device(facets, owners, counts, coords, station_ids, jones_table):
    device_index = lax.axis_index("fs").astype(jnp.int32)
    pol_index = lax.axis_index("pol")
    all_coords = lax.all_gather(coords, "fs", axis=0, tiled=False)
    own = add_up(predict(facets[0], owners, counts, all_coords, device_index))
    visible = lax.all_gather(own, "pol", axis=0, tiled=False)
    tables = jnp.concatenate(
        [
            lax.dynamic_slice_in_dim(jones_table, 4 * (pol_index // 2), 4, 0),
            lax.dynamic_slice_in_dim(jones_table, 4 * (pol_index % 2), 4, 0),
        ],
        axis=0,
    )
    return correct(visible, owners, counts, station_ids, tables, device_index)[None]


def solution(mesh):
    return jax.shard_map(
        on_device,
        mesh=mesh,
        in_specs=(
            P("pol", "fs", None, None),
            P(),
            P(),
            P(None, "fs", None, None),
            P("fs", None, None, None),
            P(),
        ),
        out_specs=P("pol", None, "fs", None, None),
        check_vma=False,
    )
```

profile of v0, /device:TPU:0, one launch (start us, length us, event | category | flops | bytes accessed | tf_op | source)
XLA Modules:
  0.0 286.1 jit_solution(6331381342462517787)
XLA Ops:
  6.5 0.0 all-gather.4.cloned.1.call-start
  6.5 0.7 all-gather.4.cloned.1.call-update
  7.3 0.1 mul.94
  7.4 0.8 constant_dynamic-slice_fusion.1
  8.2 0.6 pad_maximum_fusion.1.table_ref
  8.8 0.2 sine_convert_fusion
  8.9 0.6 pad_maximum_fusion.first_ref.second_ref
  9.6 0.1 fusion.6
  9.6 1.8 fusion.8
  11.4 41.1 %all-gather.4.cloned.1.call-done = f32[16,16,8,128]{3,2,1,0:T(8,128)} async-done(((f32[2,16,8,128]{3,2,1,0:T(8,128)}), f32[16,16,8,128]{3,2,1,0:T(8,128)}) %all-gather.4.cloned.1.call-update) | async-done | bytes 1048592 | tf_op jit(solution)/shard_map/all_gather | solution.py:387
  52.5 2.0 broadcast_in_dim.6.turn_cos_ref
  54.4 1.9 broadcast_in_dim.7.turn_sin_ref
  56.4 198.0 %shard_map.64.in_ref = bf16[8,16,2,8,128]{4,3,2,1,0:T(8,128)(2,1)} custom-call(s32[1]{0:T(128)} %bitcast.index_ref, s32[64]{0:T(128)} %owners_ref.3, s32[64]{0:T(128)} %counts_ref.3, f32[8,2,16,8,128]{4,3,2,1,0:T(8,128)} %bitcast.13, bf16[128,64]{1,0:T(8,128)(2,1)} %pad_maximum_fusion.first_ref.second_ref, ...), custom_call_target="tpu_custom_call" | custom-call | tf_op jit(solution)/shard_map/pallas_call | solution.py:237
  254.4 12.5 %shard_map.65 = f32[16,2,8,128]{3,2,1,0:T(8,128)} custom-call(bf16[8,16,2,8,128]{4,3,2,1,0:T(8,128)(2,1)} %shard_map.64.in_ref), custom_call_target="tpu_custom_call" | custom-call | tf_op jit(solution)/shard_map/pallas_call | solution.py:296
  266.9 8.1 %all-gather.1 = f32[64,2,8,128]{3,2,1,0:T(8,128)} all-gather(f32[16,2,8,128]{3,2,1,0:T(8,128)} %shard_map.65), channel_id=3, replica_groups=mesh['fs'=8,'pol'=4] {'pol'}, dimensions={0}, use_global_device_ids=true | all-gather | bytes 655360 | tf_op jit(solution)/shard_map/all_gather | solution.py:389
  275.0 4.2 %shard_map.66 = f32[2,16,8,128]{3,2,1,0:T(8,128)} custom-call(s32[1]{0:T(128)} %bitcast.index_ref, s32[64]{0:T(128)} %owners_ref.3, s32[64]{0:T(128)} %counts_ref.3, s32[16,8,128]{2,1,0:T(8,128)} %bitcast.15, s32[16,8,128]{2,1,0:T(8,128)} %bitcast.14, f32[8,512]{1,0:T(8,128)} %pad_maximum_fusion.1.table_ref, f32[4,16,2,8,128]{4,3,2,1,0:T(8,128)} %bitcast.12), custom_call_target="tpu_custom_call" | custom-call | tf_op jit(solution)/shard_map/pallas_call | solution.py:368
  (1 shorter events, 0.0 us)
Async XLA Ops:
  6.5 46.0 %all-gather.4.cloned.1.call-start = ((), (), s32[]{:S(2)}) async-start(), calls=%async_computation | async-start | bytes 1179648 | tf_op jit(solution)/shard_map/all_gather | solution.py:387
Sparse Core Ops, SparseCore 0:
  9.5 42.9 all-gather.3
where the time goes:
time: 290 us; the launch traced here: 286 us
  Pallas kernels  215 us (74%)
  waiting for transfers between devices  41.8 us (14%)
  between operations  13.4 us (5%)
  blocking collectives  8.12 us (3%)
  local copies, waits for them, and re-layouts  6.51 us (2%)
    pallas_call x1, Pallas kernels, predict(): pl.pallas_call(functools.partial(predict_kernel, facet_local, capacity),...  198 us
    all_gather x1, waiting for transfers between devices, on_device(): all_coords = lax.all_gather(coords, 'fs', axis=0, tiled=False)  41.1 us
    pallas_call x1, Pallas kernels, add_up(): pl.pallas_call(functools.partial(add_up_kernel, device_count), out_shape=...  12.5 us
    all_gather x1, blocking collectives, on_device(): visible = lax.all_gather(own, 'pol', axis=0, tiled=False)  8.12 us
  transfers between devices with their start and end apart: 1, of which 1 were waited for; matrix products, arithmetic and copies ran while one was open for 1% of the time, Pallas kernels for 0%

commit v1 on v0

--- a/solution.py
+++ b/solution.py
@@ -13,13 +13,13 @@
 S = 64
 FH = 4096
 SG = 512
-UNROLL = 2
-GROUP = 2
+UNROLL = 4
+GROUP = 4
 
 SIN_COEFS = [
-    (-1) ** i * (2.0 * math.pi) ** (2 * i + 1) / math.factorial(2 * i + 1) for i in range(9)
+    (-1) ** i * math.pi ** (2 * i + 1) / math.factorial(2 * i + 1) for i in range(6)
 ]
-COS_COEFS = [(-1) ** i * (2.0 * math.pi) ** (2 * i) / math.factorial(2 * i) for i in range(10)]
+COS_COEFS = [(-1) ** i * math.pi ** (2 * i) / math.factorial(2 * i) for i in range(7)]
 
 
 def dft_tables(length):
@@ -45,10 +45,13 @@
 
 
 def phase(position, multiple):
-    turns = position * (multiple * (1.0 / SG))
-    turns = turns - jnp.floor(turns + 0.5)
-    square = turns * turns
-    return horner(COS_COEFS, square), horner(SIN_COEFS, square) * turns
+    halves = position * (multiple * (2.0 / SG))
+    nearest = jnp.floor(halves + 0.5)
+    rest = halves - nearest
+    square = rest * rest
+    pairs = nearest * 0.5
+    flip = 1.0 - 4.0 * (pairs - jnp.floor(pairs))
+    return horner(COS_COEFS, square) * flip, horner(SIN_COEFS, square) * (rest * flip)
 
 
 def twice(left, right):
@@ -59,66 +62,95 @@
     return pltpu.roll(values, W, 1) * sign
 
 
-def predict_kernel(
-    facet_local, capacity, index_ref, owners_ref, counts_ref, coords_ref, first_ref, second_ref,
-    turn_cos_ref, turn_sin_ref, strip_ref, out_ref,
-    wide_ref, turned_ref, windows_ref, grid_ref, vis_ref, items_ref, loads_ref
+def transform_kernel(
+    first_ref, second_ref, turn_cos_ref, turn_sin_ref, strip_ref, out_ref, turned_ref, window_ref
 ):
-    facet = pl.program_id(0)
     width = 2 * W
     lanes = lax.broadcasted_iota(jnp.int32, (1, width), 1)
     sign = jnp.where(lanes < W, 1.0, -1.0)
 
-    def widen(i, carry):
-        rows = pl.ds(pl.multiple_of(i * 256, 256), 256)
-        wide_ref[rows, :] = strip_ref[0, rows, :].astype(jnp.float32)
-        return carry
-
-    lax.fori_loop(0, FH // 256, widen, 0)
-
     def first(i, carry):
-        starts = [i * GROUP + u for u in range(GROUP)]
-        data = jnp.concatenate(
-            [wide_ref[pl.ds(n, W, stride=S), :].astype(jnp.bfloat16) for n in starts], axis=1
-        )
-        both = jnp.dot(first_ref[...], data, preferred_element_type=jnp.float32)
-        for u, n in enumerate(starts):
-            part = both[:, u * width : (u + 1) * width]
-            rows = pl.ds(pl.multiple_of(n * W, W), W)
-            tc, ts = turn_cos_ref[rows, :], turn_sin_ref[rows, :]
-            straight = part[:W] * tc - part[W:] * ts
-            crossed = part[W:] * tc + part[:W] * ts
-            turned_ref[rows, :] = straight + turn_lanes(crossed, sign)
-        return carry
-
-    lax.fori_loop(0, S // GROUP, first, 0)
+        start = pl.multiple_of(i * 16, 16)
+        strips = jnp.swapaxes(strip_ref[0, :, pl.ds(start, 16), :].astype(jnp.float32), 0, 1)
+        strips = strips.astype(jnp.bfloat16)
+        for j in range(0, 16, GROUP):
+            data = jnp.concatenate([strips[j + u] for u in range(GROUP)], axis=1)
+            both = jnp.dot(first_ref[...], data, preferred_element_type=jnp.float32)
+            for u in range(GROUP):
+                n = start + j + u
+                part = both[:, u * width : (u + 1) * width]
+                tc, ts = turn_cos_ref[n], turn_sin_ref[n]
+                straight = part[:W] * tc - part[W:] * ts
+                crossed = part[W:] * tc + part[:W] * ts
+                turned_ref[n] = straight + turn_lanes(crossed, sign)
+        return carry
+
+    lax.fori_loop(0, S // 16, first, 0)
 
     def second(i, carry):
-        starts = [i * GROUP + u for u in range(GROUP)]
-        data = jnp.concatenate(
-            [turned_ref[pl.ds(k, S, stride=W), :].astype(jnp.bfloat16) for k in starts], axis=1
-        )
-        both = jnp.dot(second_ref[...], data, preferred_element_type=jnp.float32)
-        for u, k in enumerate(starts):
-            part = both[:, u * width : (u + 1) * width]
-            rows = pl.ds(pl.multiple_of(k * S, S), S)
-            windows_ref[facet, rows, :] = part[:S] + turn_lanes(part[S:], sign)
-        return carry
-
-    lax.fori_loop(0, W // GROUP, second, 0)
-
-    @pl.when(facet == facet_local - 1)
-    def _():
-        predict_all(
-            facet_local, capacity, index_ref, owners_ref, counts_ref, coords_ref, windows_ref,
-            grid_ref, vis_ref, items_ref, loads_ref
-        )
-        out_ref[...] = vis_ref[...].astype(jnp.bfloat16)
-
-
-def predict_all(
-    facet_local, capacity, index_ref, owners_ref, counts_ref, coords_ref, windows_ref,
-    grid_ref, out_ref, items_ref, loads_ref
+        start = pl.multiple_of(i * 8, 8)
+        turned = jnp.swapaxes(turned_ref[:, pl.ds(start, 8), :], 0, 1).astype(jnp.bfloat16)
+        for j in range(0, 8, GROUP):
+            data = jnp.concatenate([turned[j + u] for u in range(GROUP)], axis=1)
+            both = jnp.dot(second_ref[...], data, preferred_element_type=jnp.float32)
+            for u in range(GROUP):
+                part = both[:, u * width : (u + 1) * width]
+                window_ref[start + j + u] = part[:S] + turn_lanes(part[S:], sign)
+        return carry
+
+    lax.fori_loop(0, W // 8, second, 0)
+
+    def third(i, carry):
+        start = pl.multiple_of(i * 8, 8)
+        windows = jnp.swapaxes(window_ref[:, pl.ds(start, 8), :], 0, 1)
+        out_ref[pl.ds(start, 8), 0] = windows.astype(jnp.bfloat16)
+        return carry
+
+    lax.fori_loop(0, S // 8, third, 0)
+
+
+def turn_lanes(values, sign):
+    return pltpu.roll(values, W, 1) * sign
+
+
+def transform(strips):
+    facet_local = strips.shape[0]
+    whole = lambda *shape: pl.BlockSpec(shape, lambda f: (0,) * len(shape))
+    turns = [
+        jnp.broadcast_to(table.T[:, :, None], (S, W, 2 * W)) for table in turn_table(W, S, FH)
+    ]
+    windows = pl.pallas_call(
+        transform_kernel,
+        out_shape=jax.ShapeDtypeStruct((S, facet_local // 2, W, 4 * W), jnp.bfloat16),
+        grid=(facet_local,),
+        in_specs=[
+            whole(2 * W, W),
+            whole(2 * S, S),
+            whole(S, W, 2 * W),
+            whole(S, W, 2 * W),
+            pl.BlockSpec((1, W, S, 2 * W), lambda f: (f, 0, 0, 0)),
+        ],
+        out_specs=pl.BlockSpec((S, 1, W, 2 * W), lambda f: (0, f // 2, 0, f % 2)),
+        scratch_shapes=[
+            pltpu.VMEM((S, W, 2 * W), jnp.float32),
+            pltpu.VMEM((W, S, 2 * W), jnp.float32),
+        ],
+        compiler_params=pltpu.CompilerParams(vmem_limit_bytes=32 * 2**20),
+        cost_estimate=pl.CostEstimate(
+            flops=5 * 10**10, bytes_accessed=64 * 2**20, transcendentals=0
+        ),
+    )(
+        jnp.concatenate(dft_tables(W), axis=0),
+        jnp.concatenate(dft_tables(S), axis=0),
+        *turns,
+        strips.reshape(facet_local, W, S, 2 * W),
+    )
+    return windows.reshape(S, facet_local // 2 * W, 4 * W)
+
+
+def predict_kernel(
+    facet_local, capacity, index_ref, owners_ref, counts_ref, coords_ref, windows_ref, parts_ref,
+    out_ref, items_ref, loads_ref
 ):
     device_count = out_ref.shape[0]
     max_blocks = out_ref.shape[3]
@@ -155,17 +187,6 @@
     lax.fori_loop(0, UNROLL - 1, pad, 0)
     lane = out_ref.shape[4]
     ramp = lax.broadcasted_iota(jnp.int32, (8, lane), 0).astype(jnp.float32)
-
-    def pack(s, carry):
-        for f in range(facet_local):
-            rows = slice(f // 2 * W, (f // 2 + 1) * W)
-            cols = slice(f % 2 * 2 * W, (f % 2 + 1) * 2 * W)
-            grid_ref[s, rows, cols] = windows_ref[f, pl.ds(s, W, stride=S), :].astype(
-                jnp.bfloat16
-            )
-        return carry
-
-    lax.fori_loop(0, S, pack, 0)
 
     def one(item):
         b = item % max_blocks
@@ -176,7 +197,9 @@
         x = coords_ref[owner, 0, load, pl.ds(b, 1), :]
         y = coords_ref[owner, 1, load, pl.ds(b, 1), :]
         fine = phase(y, ramp)
-        coarse = [phase(y, ramp * 8.0), phase(y, ramp * 8.0 + 64.0)]
+        upper = phase(y, jnp.where(ramp < uppers, ramp * (2.0 * W) + col_start, 1.0 * W))
+        coarse = phase(y, ramp * 8.0)
+        coarse = [coarse, twice(coarse, (upper[0][uppers:uppers + 1], upper[1][uppers:uppers + 1]))]
         cos_rows, sin_rows, neg_rows = [], [], []
         for half in coarse:
             c, s_ = half
@@ -193,8 +216,7 @@
             ],
             axis=1,
         )
-        grid = jnp.dot(grid_ref[s], table, preferred_element_type=jnp.float32)
-        upper = phase(y, ramp * (2.0 * W) + col_start)
+        grid = jnp.dot(windows_ref[s], table, preferred_element_type=jnp.float32)
         row_coarse = phase(x, ramp * 8.0 + row_start)
         row_fine = phase(x, ramp)
         sum_real = jnp.zeros((8, lane), jnp.float32)
@@ -220,45 +242,27 @@
         return carry
 
     lax.fori_loop(0, (total + UNROLL - 1) // UNROLL, step, 0)
-
-
-def predict(strips, owners, counts, coords, device_index):
+    parts_ref[...] = out_ref[...].astype(jnp.bfloat16)
+
+
+def predict(windows, owners, counts, coords, device_index):
     device_count, _, capacity, max_blocks, lane = coords.shape
-    facet_local = strips.shape[0]
+    facet_local = windows.shape[1] // W * 2
     smem = pl.BlockSpec(memory_space=pltpu.SMEM)
-    whole = lambda *shape: pl.BlockSpec(shape, lambda f: (0,) * len(shape))
-    first = jnp.concatenate(dft_tables(W), axis=0)
-    second = jnp.concatenate(dft_tables(S), axis=0)
-    turns = [
-        jnp.broadcast_to(table.T[:, :, None], (S, W, 2 * W)).reshape(FH, 2 * W)
-        for table in turn_table(W, S, FH)
-    ]
+    vmem = pl.BlockSpec(memory_space=pltpu.VMEM)
     slots = (device_count, capacity, 2, max_blocks, lane)
     return pl.pallas_call(
         functools.partial(predict_kernel, facet_local, capacity),
         out_shape=jax.ShapeDtypeStruct(slots, jnp.bfloat16),
-        grid=(facet_local,),
-        in_specs=[
-            smem, smem, smem,
-            whole(*coords.shape),
-            whole(2 * W, W),
-            whole(2 * S, S),
-            whole(FH, 2 * W),
-            whole(FH, 2 * W),
-            pl.BlockSpec((1, FH, 2 * W), lambda f: (f, 0, 0)),
-        ],
-        out_specs=whole(*slots),
+        in_specs=[smem, smem, smem, vmem, vmem],
+        out_specs=vmem,
         scratch_shapes=[
-            pltpu.VMEM((FH, 2 * W), jnp.float32),
-            pltpu.VMEM((FH, 2 * W), jnp.float32),
-            pltpu.VMEM((facet_local, FH, 2 * W), jnp.float32),
-            pltpu.VMEM((S, facet_local // 2 * W, 4 * W), jnp.bfloat16),
             pltpu.VMEM(slots, jnp.float32),
             pltpu.SMEM((owners.shape[0] * max_blocks + UNROLL,), jnp.int32),
             pltpu.SMEM((device_count,), jnp.int32),
         ],
-        compiler_params=pltpu.CompilerParams(vmem_limit_bytes=58 * 2**20),
-    )(device_index.reshape(1), owners, counts, coords, first, second, *turns, strips)
+        compiler_params=pltpu.CompilerParams(vmem_limit_bytes=40 * 2**20),
+    )(device_index.reshape(1), owners, counts, coords, windows)
 
 
 def add_up_kernel(device_count, in_ref, out_ref, arrived_ref, send_sem, recv_sem):
@@ -385,7 +389,7 @@
     device_index = lax.axis_index("fs").astype(jnp.int32)
     pol_index = lax.axis_index("pol")
     all_coords = lax.all_gather(coords, "fs", axis=0, tiled=False)
-    own = add_up(predict(facets[0], owners, counts, all_coords, device_index))
+    own = add_up(predict(transform(facets[0]), owners, counts, all_coords, device_index))
     visible = lax.all_gather(own, "pol", axis=0, tiled=False)
     tables = jnp.concatenate(
         [

time: 290 us -> 145 us (0.50)
  Pallas kernels: 215 us -> 105 us
  waiting for transfers between devices: 41.8 us -> 0.71 us
  local copies, waits for them, and re-layouts: 6.51 us -> 14 us
    pallas_call x1, Pallas kernels: 198 us -> 43.5 us  [predict(): pl.pallas_call(functools.partial(predict_kernel, facet_local, capacity),...]
    pallas_call x0 -> x1, Pallas kernels: none -> 41.8 us  [transform(): pl.pallas_call(transform_kernel, out_shape=jax.ShapeDtypeStruct((S, facet...]
    all_gather x1, waiting for transfers between devices: 41.1 us -> 0.01 us  [on_device(): all_coords = lax.all_gather(coords, 'fs', axis=0, tiled=False)]
    unnamed x0 -> x18, local copies, waits for them, and re-layouts: none -> 12 us
    pallas_call x1, Pallas kernels: 12.5 us -> 16.2 us  [add_up(): pl.pallas_call(functools.partial(add_up_kernel, device_count), out_shape=...]
  transfers between devices with their start and end apart: 1 -> 1, of which waited for: 1 -> 0; matrix products, arithmetic and copies ran while one was open for 1% -> 2% of each run, Pallas kernels for 0% -> 29%
where the time goes in v1:
time: 145 us; the launch traced here: 143 us
  Pallas kernels  105 us (72%)
  local copies, waits for them, and re-layouts  14 us (10%)
  between operations  13.5 us (9%)
  blocking collectives  8.55 us (6%)
    pallas_call x1, Pallas kernels, predict(): pl.pallas_call(functools.partial(predict_kernel, facet_local, capacity),...  43.5 us
    pallas_call x1, Pallas kernels, transform(): pl.pallas_call(transform_kernel, out_shape=jax.ShapeDtypeStruct((S, facet...  41.8 us
    pallas_call x1, Pallas kernels, add_up(): pl.pallas_call(functools.partial(add_up_kernel, device_count), out_shape=...  16.2 us
    unnamed x18, local copies, waits for them, and re-layouts  12 us
    all_gather x1, blocking collectives, on_device(): visible = lax.all_gather(own, 'pol', axis=0, tiled=False)  8.55 us
    pallas_call x1, Pallas kernels, correct(): pl.pallas_call(correct_kernel, out_shape=jax.ShapeDtypeStruct((2, capacit...  3.76 us
  transfers between devices with their start and end apart: 1, of which 0 were waited for; matrix products, arithmetic and copies ran while one was open for 2% of the time, Pallas kernels for 29%

profile of v1, /device:TPU:0, one launch (start us, length us, event | category | flops | bytes accessed | tf_op | source)
XLA Modules:
  0.0 143.0 jit_solution(7972107968204670338)
XLA Ops:
  6.5 0.0 all-gather.4.cloned.1.call-start
  6.5 0.7 all-gather.4.cloned.1.call-update
  7.3 0.2 sine_convert_fusion
  7.4 0.1 fusion.12
  7.6 0.1 fusion.11
  7.7 0.6 broadcast_in_dim.6.turn_cos_ref
  8.3 0.6 broadcast_in_dim.7.turn_sin_ref
  8.9 0.0 copy-start.6
  8.9 3.4 %copy-done.6 = bf16[1,8,4096,128]{3,2,1,0:T(8,128)(2,1)S(1)} copy-done((bf16[1,8,4096,128]{3,2,1,0:T(8,128)(2,1)S(1)}, bf16[1,8,4096,128]{3,2,1,0:T(8,128)(2,1)}, u32[]{:S(2)}) %copy-start.6) | copy-done | bytes 8388632
  12.3 41.8 %shard_map.64 = bf16[64,4,64,256]{3,2,1,0:T(8,128)(2,1)S(1)} custom-call(bf16[128,64]{1,0:T(8,128)(2,1)S(1)} %pad_maximum_fusion.first_ref.second_ref, bf16[128,64]{1,0:T(8,128)(2,1)S(1)} %pad_maximum_fusion.first_ref.second_ref, f32[64,64,128]{2,1,0:T(8,128)S(1)} %broadcast_in_dim.6.turn_cos_ref, f32[64,64,128]{2,1,0:T(8,128)S(1)} %broadcast_in_dim.7.turn_sin_ref, ...), custom_call_target="tpu_custom_call" | custom-call | flops 49999998976 | bytes 67108864 | tf_op jit(solution)/shard_map/pallas_call | solution.py:122
  54.2 0.0 copy-start
  54.2 3.2 %copy-done = bf16[64,4,64,256]{3,2,1,0:T(8,128)(2,1)} copy-done((bf16[64,4,64,256]{3,2,1,0:T(8,128)(2,1)}, bf16[64,4,64,256]{3,2,1,0:T(8,128)(2,1)S(1)}, u32[]{:S(2)}) %copy-start) | copy-done | bytes 8388632
  57.4 0.0 copy-done.8
  57.4 0.6 pad_maximum_fusion.1.table_ref
  58.0 0.0 copy-done.7
  58.0 0.8 fusion.13
  58.8 0.0 copy-start.1
  58.8 3.4 %copy-done.1 = bf16[64,4,64,256]{3,2,1,0:T(8,128)(2,1)S(1)} copy-done((bf16[64,4,64,256]{3,2,1,0:T(8,128)(2,1)S(1)}, bf16[64,4,64,256]{3,2,1,0:T(8,128)(2,1)}, u32[]{:S(2)}) %copy-start.1) | copy-done | bytes 8388632
  62.2 1.2 copy-done.3
  63.4 43.5 %shard_map.65.in_ref = bf16[8,16,2,8,128]{4,3,2,1,0:T(8,128)(2,1)S(1)} custom-call(s32[1]{0:T(128)} %bitcast.index_ref, s32[64]{0:T(128)S(1)} %copy-done.4, s32[64]{0:T(128)S(1)} %copy-done.5, f32[8,2,16,8,128]{4,3,2,1,0:T(8,128)S(1)} %bitcast.13, bf16[64,256,256]{2,1,0:T(8,128)(2,1)S(1)} %bitcast.12), custom_call_target="tpu_custom_call" | custom-call | tf_op jit(solution)/shard_map/pallas_call | solution.py:254
  106.9 0.8 copy-done.2
  107.6 16.2 %shard_map.66 = f32[16,2,8,128]{3,2,1,0:T(8,128)} custom-call(bf16[8,16,2,8,128]{4,3,2,1,0:T(8,128)(2,1)} %copy-done.2), custom_call_target="tpu_custom_call" | custom-call | tf_op jit(solution)/shard_map/pallas_call | solution.py:300
  123.9 8.6 %all-gather.1 = f32[64,2,8,128]{3,2,1,0:T(8,128)} all-gather(f32[16,2,8,128]{3,2,1,0:T(8,128)} %shard_map.66), channel_id=3, replica_groups=mesh['fs'=8,'pol'=4] {'pol'}, dimensions={0}, use_global_device_ids=true | all-gather | bytes 655360 | tf_op jit(solution)/shard_map/all_gather | solution.py:393
  132.4 3.8 %shard_map.67 = f32[2,16,8,128]{3,2,1,0:T(8,128)} custom-call(s32[1]{0:T(128)} %bitcast.index_ref, s32[64]{0:T(128)} %owners_ref.3, s32[64]{0:T(128)} %counts_ref.3, s32[16,8,128]{2,1,0:T(8,128)} %bitcast.17, s32[16,8,128]{2,1,0:T(8,128)} %bitcast.16, f32[8,512]{1,0:T(8,128)} %pad_maximum_fusion.1.table_ref, f32[4,16,2,8,128]{4,3,2,1,0:T(8,128)} %bitcast.15), custom_call_target="tpu_custom_call" | custom-call | tf_op jit(solution)/shard_map/pallas_call | solution.py:372
  (11 shorter events, 0.0 us)
Async XLA Ops:
  6.5 52.2 %all-gather.4.cloned.1.call-start = ((), (), s32[]{:S(2)}) async-start(), calls=%async_computation | async-start | bytes 1179648 | tf_op jit(solution)/shard_map/all_gather | solution.py:391
  8.9 3.4 %copy-start.6 = (bf16[1,8,4096,128]{3,2,1,0:T(8,128)(2,1)S(1)}, bf16[1,8,4096,128]{3,2,1,0:T(8,128)(2,1)}, u32[]{:S(2)}) copy-start(bf16[1,8,4096,128]{3,2,1,0:T(8,128)(2,1)} %param.6) | copy-start | bytes 25165828
  12.3 45.1 %copy-start.8 = (f32[8,512]{1,0:T(8,128)S(1)}, f32[8,512]{1,0:T(8,128)}, u32[]{:S(2)}) copy-start(f32[8,512]{1,0:T(8,128)} %param.11) | copy-start | bytes 49156
  12.3 45.7 %copy-start.7 = (s32[16,8,2,128]{3,2,1,0:T(2,128)S(1)}, s32[16,8,2,128]{3,2,1,0:T(2,128)}, u32[]{:S(2)}) copy-start(s32[16,8,2,128]{3,2,1,0:T(2,128)} %param.10) | copy-start | bytes 393220
  12.3 46.4 %copy-start.4 = (s32[64]{0:T(128)S(1)}, s32[64]{0:T(128)}, u32[]{:S(2)}) copy-start(s32[64]{0:T(128)} %owners_ref.3) | copy-start | bytes 772
  12.3 46.4 %copy-start.5 = (s32[64]{0:T(128)S(1)}, s32[64]{0:T(128)}, u32[]{:S(2)}) copy-start(s32[64]{0:T(128)} %counts_ref.3) | copy-start | bytes 772
  54.2 3.2 %copy-start = (bf16[64,4,64,256]{3,2,1,0:T(8,128)(2,1)}, bf16[64,4,64,256]{3,2,1,0:T(8,128)(2,1)S(1)}, u32[]{:S(2)}) copy-start(bf16[64,4,64,256]{3,2,1,0:T(8,128)(2,1)S(1)} %shard_map.64) | copy-start | bytes 25165828
  58.8 3.4 %copy-start.1 = (bf16[64,4,64,256]{3,2,1,0:T(8,128)(2,1)S(1)}, bf16[64,4,64,256]{3,2,1,0:T(8,128)(2,1)}, u32[]{:S(2)}) copy-start(bf16[64,4,64,256]{3,2,1,0:T(8,128)(2,1)} %copy-done) | copy-start | bytes 25165828
  62.2 1.2 copy-start.3
  106.8 0.8 copy-start.2
Sparse Core Ops, SparseCore 0:
  9.5 43.2 all-gather.3
